TPU v7x, 32 devices: a whole 2x2x4 slice. The times are simulated.
32 devices in a mesh: groups: 2 (over y), row: 2 (over x), col: 8 (over z, core).
Axes of the slice: x: 2, y: 2, z: 4, core: 2. Of those that a mesh axis runs over, the one named last changes fastest.
Arguments:
- node_states: bfloat16 [4096, 1024], P(('groups', 'col')), parts along dimension 0, may hold values from -14 to 14
- query_weight: bfloat16 [1024, 1024], P(None, 'row'), may hold values from -1 to 1
- key_weight: bfloat16 [1024, 1024], P(None, 'row'), may hold values from -1 to 1
- value_weight: bfloat16 [1024, 1024], P(None, 'row'), may hold values from -0.1875 to 0.1875
- output_grad: bfloat16 [4096, 1024], P(('groups', 'col'), 'row'), parts along dimension 0, may hold values from -6 to 6
- pair_list: int32 [16, 32, 2], P(('groups', 'col')), parts along dimension 0, may hold values from 0 to 15, as said below
- pair_count: int32 [16], P(('groups', 'col')), parts along dimension 0, may hold values from 2 to 32, as said below
Outputs:
- attended: bfloat16 [4096, 1024], P(('groups', 'col'), 'row'), parts along dimension 0
- node_grad: float32 [4096, 1024], P(('groups', 'col'), 'row'), parts along dimension 0
- query_grad: float32 [2048, 1024], P(('groups', 'col'), 'row'), parts along dimension 0
- key_grad: float32 [2048, 1024], P(('groups', 'col'), 'row'), parts along dimension 0
- value_grad: float32 [2048, 1024], P(('groups', 'col'), 'row'), parts along dimension 0
There are 2 independent parts, one for each index of `groups`. A program takes and returns all parts, laid end to end along the dimension named above; an argument that names none is the same for every part. Nothing has to cross between parts.
Inputs may be any that keep to these rules, and one draw needn't show every extreme that they name: `pair_list`: slot p of panel c holds a query block of the panel and a key block; the first pair_count[c] slots of a panel are distinct pairs and include (q, c * 2 + q) for every query block q; later slots hold valid indices and are not listed. `pair_count`: some panel lists all 32 slots.
All inputs are finite; a program needn't handle non-finite values.
Results may differ from a plain program's by a relative error of at most 0.015.
The roundings to bfloat16 on the way count: a program that leaves them out, or rounds other values in their place, can miss the bound.
Values may be sent and summed in bfloat16 or wider, within the bound.
A program may use at most 192 MiB of HBM per device.

v0:
```python
import math
import jax
import jax.numpy as jnp
from jax import lax
from jax.sharding import PartitionSpec as P

DH = 64
BLK = 128
LOWEST = -1e30
EXACT = lax.Precision.HIGHEST


def slot_batch(pair_rows, pair_total, turn_index, width, blocks):
    start = turn_index * width
    query_block = pair_rows[:, 0]
    key_block = pair_rows[:, 1]
    slot_live = start + jnp.arange(width, dtype=jnp.int32) < pair_total
    owners = jnp.logical_and(
        query_block[:, None] == jnp.arange(blocks, dtype=jnp.int32)[None, :], slot_live[:, None]
    )
    return (query_block, key_block, slot_live, owners)


def batch_tiles(query_tiles, table_tiles, query_block, key_block, head_cols, factor):
    head_count = head_cols // DH
    width = query_block.shape[0]
    query_pick = jnp.take(query_tiles, query_block, axis=0)
    table_pick = jnp.take(table_tiles, key_block, axis=0)
    key_pick = table_pick[:, :, :head_cols].reshape(width, BLK, head_count, DH)
    value_pick = table_pick[:, :, head_cols:].reshape(width, BLK, head_count, DH)
    scores = (
        jnp.einsum("sihd,sjhd->shij", query_pick, key_pick, preferred_element_type=jnp.float32)
        * factor
    )
    return (query_pick, key_pick, value_pick, scores)


def batch_weights(scores, row_top, totals, query_block, slot_live):
    top_pick = jnp.take(row_top, query_block, axis=0)
    total_pick = jnp.take(totals, query_block, axis=0)
    weights = jnp.exp(scores - top_pick[..., None]) / total_pick[..., None]
    return jnp.where(slot_live[:, None, None, None], weights, 0.0).astype(jnp.bfloat16)


def per_device(
    node_states, query_weight, key_weight, value_weight, output_grad, pair_list, pair_count
):
    head_cols = query_weight.shape[1]
    head_count = head_cols // DH
    panel_rows = node_states.shape[0]
    blocks = panel_rows // BLK
    factor = 1.0 / math.sqrt(DH)
    pair_rows = pair_list[0]
    pair_total = pair_count[0]
    width = math.gcd(pair_rows.shape[0], 32)
    turns = (pair_total + width - 1) // width
    queries = jnp.dot(node_states, query_weight, preferred_element_type=jnp.float32).astype(
        jnp.bfloat16
    )
    keys_here = jnp.dot(node_states, key_weight, preferred_element_type=jnp.float32).astype(
        jnp.bfloat16
    )
    values_here = jnp.dot(node_states, value_weight, preferred_element_type=jnp.float32).astype(
        jnp.bfloat16
    )
    local_table = jnp.concatenate([keys_here, values_here], axis=1)
    key_table = lax.all_gather(local_table, "col", axis=0, tiled=True)
    key_blocks_all = key_table.shape[0] // BLK
    query_tiles = queries.reshape(blocks, BLK, head_count, DH)
    table_tiles = key_table.reshape(key_blocks_all, BLK, 2 * head_cols)

    def stats_turn(turn_index, state_pair):
        row_top, totals = state_pair
        query_block, key_block, slot_live, owners = slot_batch(
            pair_rows, pair_total, turn_index, width, blocks
        )
        scores = batch_tiles(query_tiles, table_tiles, query_block, key_block, head_cols, factor)[3]
        pair_top = jnp.max(scores, axis=3)
        block_top = jnp.max(jnp.where(owners[:, :, None, None], pair_top[:, None], LOWEST), axis=0)
        new_top = jnp.maximum(row_top, block_top)
        top_pick = jnp.take(new_top, query_block, axis=0)
        exp_terms = jnp.where(
            slot_live[:, None, None, None], jnp.exp(scores - top_pick[..., None]), 0.0
        )
        added = jnp.einsum(
            "sn,shi->nhi", owners.astype(jnp.float32), jnp.sum(exp_terms, axis=3), precision=EXACT
        )
        totals = totals * jnp.exp(row_top - new_top) + added
        return (new_top, totals)

    start_top = jnp.full((blocks, head_count, BLK), LOWEST, jnp.float32)
    start_total = jnp.zeros((blocks, head_count, BLK), jnp.float32)
    row_top, totals = lax.fori_loop(0, turns, stats_turn, (start_top, start_total))

    def attend_turn(turn_index, output):
        query_block, key_block, slot_live, owners = slot_batch(
            pair_rows, pair_total, turn_index, width, blocks
        )
        query_pick, key_pick, value_pick, scores = batch_tiles(
            query_tiles, table_tiles, query_block, key_block, head_cols, factor
        )
        weights = batch_weights(scores, row_top, totals, query_block, slot_live)
        update = jnp.einsum(
            "shij,sjhd->sihd", weights, value_pick, preferred_element_type=jnp.float32
        )
        return output + jnp.einsum(
            "sn,sihd->nihd", owners.astype(jnp.float32), update, precision=EXACT
        )

    output = lax.fori_loop(
        0, turns, attend_turn, jnp.zeros((blocks, BLK, head_count, DH), jnp.float32)
    )
    attended = output.reshape(panel_rows, head_cols).astype(jnp.bfloat16)
    grad_tiles = output_grad.reshape(blocks, BLK, head_count, DH)
    deltas = jnp.sum(grad_tiles.astype(jnp.float32) * output, axis=3)
    back_table = lax.all_gather(local_table, "col", axis=0, tiled=True)
    back_tiles = back_table.reshape(key_blocks_all, BLK, 2 * head_cols)

    def backward_turn(turn_index, state_pair):
        grad_rows, key_grads = state_pair
        query_block, key_block, slot_live, owners = slot_batch(
            pair_rows, pair_total, turn_index, width, blocks
        )
        query_pick, key_pick, value_pick, scores = batch_tiles(
            query_tiles, back_tiles, query_block, key_block, head_cols, factor
        )
        weights = batch_weights(scores, row_top, totals, query_block, slot_live)
        grad_pick = jnp.take(grad_tiles, query_block, axis=0)
        value_part = jnp.einsum(
            "shij,sihd->sjhd", weights, grad_pick, preferred_element_type=jnp.float32
        )
        prob_grad = jnp.einsum(
            "sihd,sjhd->shij", grad_pick, value_pick, preferred_element_type=jnp.float32
        )
        delta_pick = jnp.transpose(jnp.take(deltas, query_block, axis=0), (0, 2, 1))
        score_grad = (weights.astype(jnp.float32) * (prob_grad - delta_pick[..., None])).astype(
            jnp.bfloat16
        )
        query_part = (
            jnp.einsum("shij,sjhd->sihd", score_grad, key_pick, preferred_element_type=jnp.float32)
            * factor
        )
        key_part = (
            jnp.einsum(
                "shij,sihd->sjhd", score_grad, query_pick, preferred_element_type=jnp.float32
            )
            * factor
        )
        grad_rows = grad_rows + jnp.einsum(
            "sn,sihd->nihd", owners.astype(jnp.float32), query_part, precision=EXACT
        )
        rows_update = jnp.concatenate(
            [key_part.reshape(width, BLK, head_cols), value_part.reshape(width, BLK, head_cols)],
            axis=2,
        )
        key_grads = key_grads + jax.ops.segment_sum(
            rows_update, key_block, num_segments=key_blocks_all
        )
        return (grad_rows, key_grads)

    start_rows = jnp.zeros((blocks, BLK, head_count, DH), jnp.float32)
    start_keys = jnp.zeros((key_blocks_all, BLK, 2 * head_cols), jnp.float32)
    grad_rows, key_grads = lax.fori_loop(0, turns, backward_turn, (start_rows, start_keys))
    key_grads = key_grads.reshape(key_blocks_all * BLK, 2 * head_cols)
    pair_grads = lax.psum_scatter(
        key_grads.astype(jnp.bfloat16), "col", scatter_dimension=0, tiled=True
    ).astype(jnp.float32)
    query_rows_grad = grad_rows.reshape(panel_rows, head_cols).astype(jnp.bfloat16)
    key_rows_grad = pair_grads[:, :head_cols].astype(jnp.bfloat16)
    value_rows_grad = pair_grads[:, head_cols:].astype(jnp.bfloat16)
    contract = (((1,), (1,)), ((), ()))
    partial_sum = lax.dot_general(
        query_rows_grad, query_weight, contract, preferred_element_type=jnp.float32
    )
    partial_sum = partial_sum + lax.dot_general(
        key_rows_grad, key_weight, contract, preferred_element_type=jnp.float32
    )
    partial_sum = partial_sum + lax.dot_general(
        value_rows_grad, value_weight, contract, preferred_element_type=jnp.float32
    )
    node_grad = lax.psum_scatter(
        partial_sum.astype(jnp.bfloat16), "row", scatter_dimension=1, tiled=True
    ).astype(jnp.float32)
    over_nodes = (((0,), (0,)), ((), ()))
    query_term = lax.dot_general(
        node_states, query_rows_grad, over_nodes, preferred_element_type=jnp.float32
    )
    key_term = lax.dot_general(
        node_states, key_rows_grad, over_nodes, preferred_element_type=jnp.float32
    )
    value_term = lax.dot_general(
        node_states, value_rows_grad, over_nodes, preferred_element_type=jnp.float32
    )
    query_grad, key_grad, value_grad = (
        lax.psum_scatter(
            query_term.astype(jnp.bfloat16), "col", scatter_dimension=0, tiled=True
        ).astype(jnp.float32),
        lax.psum_scatter(
            key_term.astype(jnp.bfloat16), "col", scatter_dimension=0, tiled=True
        ).astype(jnp.float32),
        lax.psum_scatter(
            value_term.astype(jnp.bfloat16), "col", scatter_dimension=0, tiled=True
        ).astype(jnp.float32),
    )
    return (attended, node_grad, query_grad, key_grad, value_grad)


def solution(mesh):
    return jax.shard_map(
        per_device,
        mesh=mesh,
        in_specs=(
            P(("groups", "col"), None),
            P(None, "row"),
            P(None, "row"),
            P(None, "row"),
            P(("groups", "col"), "row"),
            P(("groups", "col"), None, None),
            P(("groups", "col")),
        ),
        out_specs=(
            P(("groups", "col"), "row"),
            P(("groups", "col"), "row"),
            P(("groups", "col"), "row"),
            P(("groups", "col"), "row"),
            P(("groups", "col"), "row"),
        ),
        check_vma=False,
    )
```

profile of v0, /device:TPU:0, one launch (start us, length us, event | category | flops | bytes accessed | tf_op | source)
XLA Modules:
  0.0 593.4 jit_solution(17759031465043939440)
XLA Ops:
  16.7 45.1 %all-gather.2.cloned.1.call-done = bf16[2048,1024]{1,0:T(8,128)(2,1)} async-done(((bf16[256,1024]{1,0:T(8,128)(2,1)}), bf16[2048,1024]{1,0:T(8,128)(2,1)}) %all-gather.2.cloned.1.call-update) | async-done | bytes 4194320 | tf_op jit(solution)/shard_map/all_gather | solution.py:67
  61.9 55.4 %while.34 = (s32[]{:T(128)}, f32[2,8,128]{2,0,1:T(2,128)S(1)}, f32[2,8,128]{2,0,1:T(2,128)S(1)}, s32[]{:T(128)}, s32[32,2]{0,1:T(2,128)S(1)}, /*index=5*/s32[]{:...) while((s32[]{:T(128)}, f32[2,8,128]{2,0,1:T(2,128)S(1)}, ...), condition=%wide.region_4.8_spmd, body=%wide.region_0.7_spmd.sunk | while | flops 567124544 | bytes 93563064 | solution.py:93
  93.3 12.3 %multiply_reduce_fusion.3 = (f32[32,8,128]{2,1,0:T(8,128)S(1)}, f32[32,8,128,128]{2,3,1,0:T(8,128)}) fusion(bf16[32,128,8,64]{1,3,2,0:T(8,128)(2,1)} %bitcast.184, bf16[32,128,8,64]{3,2,1,0:T(8,128)(2,1)} %broadcast_select_fusion.19), kind=kOutput, calls=%fused_computation.15.clone.1 | convolution fusion | flops 545226752 | bytes 25296896 | tf_op jit(solution)/shard_map/while/body/sihd,sjhd->shij/dot_general | solution.py:32
  106.4 10.7 %select_reduce_fusion.5 = f32[32,8,128]{2,1,0:T(8,128)S(1)} fusion(f32[32,8,128,128]{2,3,1,0:T(8,128)} %get-tuple-element.622, f32[32,8,128]{2,1,0:T(8,128)S(1)} %broadcast_select_fusion.20, pred[32]{0:T(512)(128)(4,1)S(1)} %get-tuple-element.621), kind=kLoop, calls=%fused_computation.14.clone.1 | loop fusion | flops 16744448 | bytes 17039392 | tf_op jit(solution)/shard_map/while/body/reduce_sum | solution.py:86
  117.5 91.5 %while.35 = (s32[]{:T(128)}, f32[2,128,8,64]{1,0,3,2:T(2,128)S(1)}, s32[]{:T(128)}, s32[32,2]{0,1:T(2,128)S(1)}, s32[]{:T(128)}, /*index=5*/bf16[16,128,1024]{2,...) while((s32[]{:T(128)}, f32[2,128,8,64]{1,0,3,2:T(2,128)S(1)}, ...), condition=%wide.region_6.10_spmd, body=%wide.region_5.9_spmd.sunk | while | flops 1151535744 | bytes 115615744 | solution.py:110
  165.6 14.3 %fusion.117 = f32[32,128,8,64]{1,3,2,0:T(8,128)} fusion(bf16[32,128,8,64]{1,3,2,0:T(8,128)(2,1)} %bitcast.188, bf16[32,128,8,64]{1,3,2,0:T(8,128)(2,1)} %bitcast.189, bf16[32,128,8,64]{3,2,1,0:T(8,128)(2,1)} %broadcast_select_fusion.22, f32[32,8,128]{2,1,0:T(8,128)S(1)} %get-tuple-element.638, f32[32,8,128]{2,1,0:T(8,128)S(1)} %get-tuple-element.639, ...), kind=kOutput, calls=%fused_computation.42.clone.2 | convolution fusion | flops 1094713344 | bytes 21233696 | tf_op jit(solution)/shard_map/while/body/shij,sjhd->sihd/dot_general | solution.py:103
  179.9 11.3 %fusion.118 = f32[2,128,8,64]{1,0,3,2:T(2,128)S(1)} fusion(f32[2,128,8,64]{1,0,3,2:T(2,128)S(1)} %get-tuple-element.709, f32[32,128,8,64]{1,3,2,0:T(8,128)} %fusion.117, pred[32]{0:T(512)(128)(4,1)S(1)} %get-tuple-element.640, s32[32]{0:T(128)S(1)} %slice_bitcast_fusion.8), kind=kOutput, calls=%fused_computation.43.clone.1 | convolution fusion | flops 50462848 | bytes 9437344 | tf_op jit(solution)/shard_map/while/body/sn,sihd->nihd/dot_general | solution.py:106
  214.4 198.7 %while.36 = (s32[]{:T(128)}, f32[2,128,8,64]{1,0,3,2:T(2,128)S(1)}, f32[16,128,1024]{2,1,0:T(8,128)}, s32[]{:T(128)}, s32[32,2]{0,1:T(2,128)S(1)}, /*index=5*/s3...) while((s32[]{:T(128)}, f32[2,128,8,64]{1,0,3,2:T(2,128)S(1)}, ...), condition=%wide.region_10.14_spmd, body=%wide.region_8.13_spmd.sunk | while | flops 2793639936 | bytes 384713920 | solution.py:163
  260.3 11.6 %broadcast_select_fusion.25 = (bf16[32,128,8,64]{3,2,1,0:T(8,128)(2,1)}, bf16[32,128,8,64]{3,2,1,0:T(8,128)(2,1)}) fusion(bf16[32,128,8,64]{3,2,1,0:T(8,128)(2,1)} %gather_fusion.8, pred[32]{0:T(512)(128)(4,1)S(1)} %get-tuple-element.657, bf16[32,128,8,64]{3,2,1,0:T(8,128)(2,1)} %gather_fusion.9), kind=kLoop, calls=%fused_computation.68.clone.1 | loop fusion | flops 4194304 | bytes 16777248 | tf_op jit(solution)/shard_map/while/body/jit(_take)/select_n | solution.py:128
  271.9 9.0 %copy.232 = bf16[32,128,8,64]{1,3,2,0:T(8,128)(2,1)} copy(bf16[32,128,8,64]{3,2,1,0:T(8,128)(2,1)} %get-tuple-element.658) | data formatting | bytes 8388608 | tf_op jit(solution)/shard_map/while/body/jit(_take)/select_n | solution.py:27
  280.9 9.0 %copy.233 = bf16[32,128,8,64]{1,3,2,0:T(8,128)(2,1)} copy(bf16[32,128,8,64]{3,2,1,0:T(8,128)(2,1)} %get-tuple-element.662) | data formatting | bytes 8388608 | tf_op jit(solution)/shard_map/while/body/jit(_take)/select_n | solution.py:128
  290.0 15.2 %select_convert_fusion.3 = bf16[32,8,128,128]{3,2,1,0:T(8,128)(2,1)S(1)} fusion(bf16[32,128,8,64]{1,3,2,0:T(8,128)(2,1)} %copy.232, bf16[32,128,8,64]{1,3,2,0:T(8,128)(2,1)} %bitcast.186, f32[32,8,128]{2,1,0:T(8,128)S(1)} %get-tuple-element.659, f32[32,8,128]{2,1,0:T(8,128)S(1)} %get-tuple-element.660, pred[32]{0:T(512)(128)(4,1)S(1)} %get-tuple-element.661), kind=kOutput, calls=%fused_computation.64.clone.1 | convolution fusion | flops 557842432 | bytes 17039392 | tf_op jit(solution)/shard_map/while/body/sihd,sjhd->shij/dot_general | solution.py:32
  305.2 8.8 %multiply_convert_fusion.2 = bf16[32,8,128,128]{3,2,1,0:T(8,128)(2,1)} fusion(bf16[32,8,128,128]{3,2,1,0:T(8,128)(2,1)S(1)} %select_convert_fusion.3, bf16[32,128,8,64]{1,3,2,0:T(8,128)(2,1)S(1)} %copy-done.2, bf16[32,128,8,64]{1,3,2,0:T(8,128)(2,1)S(1)} %bitcast.185, f32[32,8,128]{2,1,0:T(8,128)S(1)} %select_bitcast_fusion.2), kind=kOutput, calls=%fused_computation.63.clone.1 | convolution fusion | flops 553648128 | bytes 25296896 | tf_op jit(solution)/shard_map/while/body/sihd,sjhd->shij/dot_general | solution.py:132
  318.4 9.0 %copy.235 = f32[32,128,512]{2,1,0:T(8,128)} copy(f32[32,128,512]{1,2,0:T(8,128)} %bitcast.183) | data formatting | bytes 16777216 | tf_op jit(solution)/shard_map/while/body/reshape | solution.py:153
  327.4 10.2 %broadcast_multiply_fusion.2 = f32[32,8,64,128]{3,2,1,0:T(8,128)} fusion(bf16[32,128,8,64]{1,3,2,0:T(8,128)(2,1)} %copy.232, bf16[32,8,128,128]{3,2,1,0:T(8,128)(2,1)} %multiply_convert_fusion.2), kind=kOutput, calls=%fused_computation.71.clone.1 | convolution fusion | flops 538968064 | bytes 20971520 | tf_op jit(solution)/shard_map/while/body/shij,sihd->sjhd/dot_general | solution.py:144
  337.6 10.5 %multiply_bitcast_fusion.2 = f32[32,128,8,64]{1,3,2,0:T(8,128)S(1)} fusion(bf16[32,128,8,64]{1,3,2,0:T(8,128)(2,1)} %bitcast.187, bf16[32,8,128,128]{3,2,1,0:T(8,128)(2,1)} %multiply_convert_fusion.2), kind=kOutput, calls=%fused_computation.67.clone.1 | convolution fusion | flops 538968064 | bytes 20971520 | tf_op jit(solution)/shard_map/while/body/shij,sjhd->sihd/dot_general | solution.py:140
  356.5 9.0 %copy.236 = f32[32,128,512]{2,1,0:T(8,128)} copy(f32[32,128,512]{1,2,0:T(8,128)} %bitcast.182) | data formatting | bytes 16777216 | tf_op jit(solution)/shard_map/while/body/reshape | solution.py:153
  365.5 11.7 %pad_maximum_fusion.3 = f32[32,128,1024]{2,1,0:T(8,128)} fusion(f32[32,128,512]{2,1,0:T(8,128)} %copy.235, f32[32,128,512]{2,1,0:T(8,128)} %copy.236), kind=kLoop, calls=%fused_computation.62.clone.1 | loop fusion | flops 4194304 | bytes 33554432 | tf_op jit(solution)/shard_map/while/body/concatenate | solution.py:152
  377.3 35.7 %scatter_fusion = f32[16,128,1024]{2,1,0:T(8,128)} fusion(f32[16,128,1024]{2,1,0:T(8,128)} %get-tuple-element.746, s32[32]{0:T(128)S(1)} %get-tuple-element.666, f32[32,128,1024]{2,1,0:T(8,128)} %pad_maximum_fusion.3), kind=kCustom, calls=%fused_computation.13.clone.1 | custom fusion | flops 4194304 | bytes 50331776 | tf_op jit(solution)/shard_map/while/body/scatter-add | solution.py:156
  421.8 46.7 %reduce-scatter.12.cloned.1.call-done = bf16[256,1024]{1,0:T(8,128)(2,1)} async-done(((bf16[2048,1024]{1,0:T(8,128)(2,1)}), bf16[256,1024]{1,0:T(8,128)(2,1)}) %reduce-scatter.12.cloned.1.call-update) | async-done | bytes 524304 | tf_op jit(solution)/shard_map/reduce_scatter | solution.py:165
  478.6 22.8 %reduce-scatter.16.cloned.1.call-done = bf16[128,512]{1,0:T(8,128)(2,1)} async-done(((bf16[1024,512]{1,0:T(8,128)(2,1)}), bf16[128,512]{1,0:T(8,128)(2,1)}) %reduce-scatter.16.cloned.1.call-update) | async-done | bytes 131088
  503.2 13.6 %reduce-scatter.14.cloned.1.call-done = bf16[256,512]{1,0:T(8,128)(2,1)} async-done(((bf16[256,1024]{1,0:T(8,128)(2,1)}), bf16[256,512]{1,0:T(8,128)(2,1)}) %reduce-scatter.14.cloned.1.call-update) | async-done | bytes 262160 | tf_op jit(solution)/shard_map/reduce_scatter | solution.py:181
  518.7 32.8 %reduce-scatter.18.cloned.1.call-done = bf16[128,512]{1,0:T(8,128)(2,1)} async-done(((bf16[1024,512]{1,0:T(8,128)(2,1)}), bf16[128,512]{1,0:T(8,128)(2,1)}) %reduce-scatter.18.cloned.1.call-update) | async-done | bytes 131088
  553.3 31.1 %reduce-scatter.20.cloned.1.call-done = bf16[128,512]{1,0:T(8,128)(2,1)} async-done(((bf16[1024,512]{1,0:T(8,128)(2,1)}), bf16[128,512]{1,0:T(8,128)(2,1)}) %reduce-scatter.20.cloned.1.call-update) | async-done | bytes 131088
  (125 shorter events, 179.1 us)
Async XLA Ops:
  7.2 6.6 %copy-start = (bf16[1024,512]{1,0:T(8,128)(2,1)S(1)}, bf16[1024,512]{1,0:T(8,128)(2,1)}, u32[]{:S(2)}) copy-start(bf16[1024,512]{1,0:T(8,128)(2,1)} %param.20) | copy-start | bytes 3145732
  7.2 54.7 %copy-start.9 = (s32[1,32,2]{1,2,0:T(2,128)S(1)}, s32[1,32,2]{1,2,0:T(2,128)}, u32[]{:S(2)}) copy-start(s32[1,32,2]{1,2,0:T(2,128)} %param.24) | copy-start | bytes 772
  7.2 54.7 %all-gather.2.cloned.1.call-start = ((), (), s32[]{:S(2)}) async-start(), calls=%async_computation.5 | async-start | bytes 4718592 | tf_op jit(solution)/shard_map/all_gather | solution.py:67
  11.9 456.7 %reduce-scatter.12.cloned.1.call-start = ((), (), s32[]{:S(2)}) async-start(), calls=%async_computation.6 | async-start | bytes 4718592 | tf_op jit(solution)/shard_map/reduce_scatter | solution.py:165
  13.7 48.1 %copy-start.5 = (bf16[2,128,8,64]{1,0,3,2:T(2,128)(2,1)}, bf16[2,128,8,64]{1,0,3,2:T(2,128)(2,1)S(1)}, u32[]{:S(2)}) copy-start(bf16[2,128,8,64]{1,0,3,2:T(2,128)(2,1)S(1)} %reshape.142) | copy-start | bytes 786436
  117.4 91.5 %copy-start.6 = (bf16[2,128,8,64]{1,0,3,2:T(2,128)(2,1)S(1)}, bf16[2,128,8,64]{1,0,3,2:T(2,128)(2,1)}, u32[]{:S(2)}) copy-start(bf16[2,128,8,64]{1,0,3,2:T(2,128)(2,1)} %copy-done.5) | copy-start | bytes 786436
  208.9 5.5 copy-start.1
  214.4 0.7 copy-start.10
  290.0 15.2 %copy-start.2 = (bf16[32,128,8,64]{1,3,2,0:T(8,128)(2,1)S(1)}, bf16[32,128,8,64]{1,3,2,0:T(8,128)(2,1)}, u32[]{:S(2)}) copy-start(bf16[32,128,8,64]{1,3,2,0:T(8,128)(2,1)} %copy.233) | copy-start | bytes 12582916 | tf_op jit(solution)/shard_map/while
  290.0 15.2 %copy-start.3 = (bf16[32,128,512]{1,2,0:T(8,128)(2,1)S(1)}, bf16[32,128,512]{1,2,0:T(8,128)(2,1)}, u32[]{:S(2)}) copy-start(bf16[32,128,512]{1,2,0:T(8,128)(2,1)} %copy.234) | copy-start | bytes 12582916 | tf_op jit(solution)/shard_map/while
  377.3 35.7 %copy-start.11 = (s32[32,2]{0,1:T(2,128)S(1)}, s32[32,2]{0,1:T(2,128)}, u32[]{:S(2)}) copy-start(s32[32,2]{0,1:T(2,128)} %copy-done.10) | copy-start | bytes 772 | tf_op jit(solution)/shard_map/while
  413.1 6.3 %copy-start.4 = (bf16[256,1024]{1,0:T(8,128)(2,1)S(1)}, bf16[256,1024]{1,0:T(8,128)(2,1)}, u32[]{:S(2)}) copy-start(bf16[256,1024]{1,0:T(8,128)(2,1)} %param.19) | copy-start | bytes 1572868
  419.2 82.1 %reduce-scatter.16.cloned.1.call-start = ((), (), s32[]{:S(2)}) async-start(), calls=%async_computation.8 | async-start | bytes 1179648
  421.3 95.6 %reduce-scatter.14.cloned.1.call-start = ((), (), s32[]{:S(2)}) async-start(), calls=%async_computation.7 | async-start | bytes 786432 | tf_op jit(solution)/shard_map/reduce_scatter | solution.py:181
  421.8 55.9 %copy-start.8 = (bf16[2,128,8,64]{1,0,3,2:T(2,128)(2,1)S(1)}, bf16[2,128,8,64]{1,0,3,2:T(2,128)(2,1)}, u32[]{:S(2)}) copy-start(bf16[2,128,8,64]{1,0,3,2:T(2,128)(2,1)} %get-tuple-element.426) | copy-start | bytes 786436
  468.6 7.3 %copy-start.7 = (bf16[256,1024]{1,0:T(8,128)(2,1)S(1)}, bf16[256,1024]{1,0:T(8,128)(2,1)}, u32[]{:S(2)}) copy-start(bf16[256,1024]{1,0:T(8,128)(2,1)} %reduce-scatter.12.cloned.1.call-done) | copy-start | bytes 1572868
  473.0 78.4 %reduce-scatter.18.cloned.1.call-start = ((), (), s32[]{:S(2)}) async-start(), calls=%async_computation.9 | async-start | bytes 1179648
  475.8 108.5 %reduce-scatter.20.cloned.1.call-start = ((), (), s32[]{:S(2)}) async-start(), calls=%async_computation.10 | async-start | bytes 1179648
Sparse Core Ops, SparseCore 0:
  12.0 49.8 all-gather.1
  419.3 49.1 reduce-scatter.11
  470.8 30.4 reduce-scatter.15
  504.0 12.7 reduce-scatter.13
  519.1 32.2 reduce-scatter.17
  553.6 30.6 reduce-scatter.19
where the time goes:
time: 605 us; the launch traced here: 593 us
  waiting for transfers between devices  192 us (32%)
  local copies, waits for them, and re-layouts  142 us (23%)
  other arithmetic  117 us (19%)
  matrix products  108 us (18%)
  loops' own time  18.5 us (3%)
  between operations  15.4 us (3%)
    unnamed x9, waiting for transfers between devices  86.7 us
    reduce_scatter x1, waiting for transfers between devices, per_device(): lax.psum_scatter(key_grads.astype(jnp.bfloat16), 'col', scatter_dimension...  46.7 us
    all_gather x1, waiting for transfers between devices, per_device(): key_table = lax.all_gather(local_table, 'col', axis=0, tiled=True)  45.1 us
    scatter-add x1, other arithmetic, backward_turn(): jax.ops.segment_sum(rows_update, key_block, num_segments=key_blocks_all)  35.7 us
    dot_general x2, matrix products, batch_tiles(): jnp.einsum('sihd,sjhd->shij', query_pick, key_pick, preferred_element_typ...  27.5 us
    slice x4, local copies, waits for them, and re-layouts, batch_tiles(): key_pick = table_pick[:, :, :head_cols].reshape(width, BLK, head_count, DH)  25.2 us
    gather x3, local copies, waits for them, and re-layouts, batch_tiles(): table_pick = jnp.take(table_tiles, key_block, axis=0)  21.6 us
    select_n x3, other arithmetic, batch_tiles(): table_pick = jnp.take(table_tiles, key_block, axis=0)  19.5 us
  transfers between devices with their start and end apart: 6, of which 6 were waited for; matrix products, arithmetic and copies ran while one was open for 4% of the time, Pallas kernels for 0%

commit v1 on v0

--- a/solution.py
+++ b/solution.py
@@ -64,7 +64,12 @@
         jnp.bfloat16
     )
     local_table = jnp.concatenate([keys_here, values_here], axis=1)
-    key_table = lax.all_gather(local_table, "col", axis=0, tiled=True)
+    ring = [local_table]
+    for hop in range(7):
+        ring.append(lax.ppermute(ring[-1], "col", [(dev, (dev + 1) % 8) for dev in range(8)]))
+    key_table = jnp.roll(
+        jnp.concatenate(ring[::-1], axis=0), (lax.axis_index("col") + 1) * ring[0].shape[0], axis=0
+    )
     key_blocks_all = key_table.shape[0] // BLK
     query_tiles = queries.reshape(blocks, BLK, head_count, DH)
     table_tiles = key_table.reshape(key_blocks_all, BLK, 2 * head_cols)

time: 605 us -> 635 us (1.050)
  waiting for transfers between devices: 192 us -> 214 us
  local copies, waits for them, and re-layouts: 142 us -> 156 us
    ppermute x0 -> x7, waiting for transfers between devices: none -> 67.1 us  [per_device(): lax.ppermute(ring[-1], 'col', [(dev, (dev + 1) % 8) for dev in range(8)])]
    all_gather x1, waiting for transfers between devices: 45.1 us -> 0.01 us  [per_device(): back_table = lax.all_gather(local_table, 'col', axis=0, tiled=True)]
    unnamed x28 -> x56, local copies, waits for them, and re-layouts: 11.5 us -> 21.8 us
  transfers between devices with their start and end apart: 6 -> 13, of which waited for: 6 -> 12; matrix products, arithmetic and copies ran while one was open for 4% -> 26% of each run, Pallas kernels for 0% -> 0%
where the time goes in v1:
time: 635 us; the launch traced here: 630 us
  waiting for transfers between devices  214 us (34%)
  local copies, waits for them, and re-layouts  156 us (25%)
  other arithmetic  117 us (18%)
  matrix products  108 us (17%)
  loops' own time  18.4 us (3%)
  between operations  15.4 us (2%)
    unnamed x9, waiting for transfers between devices  86.9 us
    ppermute x7, waiting for transfers between devices, per_device(): lax.ppermute(ring[-1], 'col', [(dev, (dev + 1) % 8) for dev in range(8)])  67.1 us
    reduce_scatter x1, waiting for transfers between devices, per_device(): lax.psum_scatter(key_grads.astype(jnp.bfloat16), 'col', scatter_dimension...  46.2 us
    scatter-add x1, other arithmetic, backward_turn(): jax.ops.segment_sum(rows_update, key_block, num_segments=key_blocks_all)  35.7 us
    dot_general x2, matrix products, batch_tiles(): jnp.einsum('sihd,sjhd->shij', query_pick, key_pick, preferred_element_typ...  26.8 us
    slice x4, local copies, waits for them, and re-layouts, batch_tiles(): key_pick = table_pick[:, :, :head_cols].reshape(width, BLK, head_count, DH)  25.1 us
    gather x3, local copies, waits for them, and re-layouts, batch_tiles(): table_pick = jnp.take(table_tiles, key_block, axis=0)  21.8 us
    unnamed x56, local copies, waits for them, and re-layouts  21.8 us
  transfers between devices with their start and end apart: 13, of which 12 were waited for; matrix products, arithmetic and copies ran while one was open for 26% of the time, Pallas kernels for 0%

profile of v1, /device:TPU:0, one launch (start us, length us, event | category | flops | bytes accessed | tf_op | source)
XLA Modules:
  0.0 629.6 jit_solution(4240358302383549877)
XLA Ops:
  11.5 10.9 %collective-permute-done = bf16[256,1024]{1,0:T(8,128)(2,1)S(1)} collective-permute-done((bf16[256,1024]{1,0:T(8,128)(2,1)S(1)}, bf16[256,1024]{1,0:T(8,128)(2,1)S(1)}, u32[]{:S(2)}, u32[]{:S(2)}) %collective-permute-start) | collective-permute-done | bytes 524320 | tf_op jit(solution)/shard_map/ppermute | solution.py:69
  22.4 10.4 %collective-permute-done.1 = bf16[256,1024]{1,0:T(8,128)(2,1)S(1)} collective-permute-done((bf16[256,1024]{1,0:T(8,128)(2,1)S(1)}, bf16[256,1024]{1,0:T(8,128)(2,1)S(1)}, u32[]{:S(2)}, u32[]{:S(2)}) %collective-permute-start.1) | collective-permute-done | bytes 524320 | tf_op jit(solution)/shard_map/ppermute | solution.py:69
  32.9 10.4 %collective-permute-done.2 = bf16[256,1024]{1,0:T(8,128)(2,1)S(1)} collective-permute-done((bf16[256,1024]{1,0:T(8,128)(2,1)S(1)}, bf16[256,1024]{1,0:T(8,128)(2,1)S(1)}, u32[]{:S(2)}, u32[]{:S(2)}) %collective-permute-start.2) | collective-permute-done | bytes 524320 | tf_op jit(solution)/shard_map/ppermute | solution.py:69
  44.0 10.4 %collective-permute-done.3 = bf16[256,1024]{1,0:T(8,128)(2,1)S(1)} collective-permute-done((bf16[256,1024]{1,0:T(8,128)(2,1)S(1)}, bf16[256,1024]{1,0:T(8,128)(2,1)S(1)}, u32[]{:S(2)}, u32[]{:S(2)}) %collective-permute-start.3) | collective-permute-done | bytes 524320 | tf_op jit(solution)/shard_map/ppermute | solution.py:69
  55.2 10.4 %collective-permute-done.4 = bf16[256,1024]{1,0:T(8,128)(2,1)S(1)} collective-permute-done((bf16[256,1024]{1,0:T(8,128)(2,1)S(1)}, bf16[256,1024]{1,0:T(8,128)(2,1)S(1)}, u32[]{:S(2)}, u32[]{:S(2)}) %collective-permute-start.4) | collective-permute-done | bytes 524320 | tf_op jit(solution)/shard_map/ppermute | solution.py:69
  66.4 10.5 %collective-permute-done.5 = bf16[256,1024]{1,0:T(8,128)(2,1)} collective-permute-done((bf16[256,1024]{1,0:T(8,128)(2,1)S(1)}, bf16[256,1024]{1,0:T(8,128)(2,1)}, u32[]{:S(2)}, u32[]{:S(2)}) %collective-permute-start.5) | collective-permute-done | bytes 524320 | tf_op jit(solution)/shard_map/ppermute | solution.py:69
  98.2 55.5 %while.34 = (s32[]{:T(128)}, f32[2,8,128]{2,0,1:T(2,128)S(1)}, f32[2,8,128]{2,0,1:T(2,128)S(1)}, s32[]{:T(128)}, s32[32,2]{0,1:T(2,128)S(1)}, /*index=5*/s32[]{:...) while((s32[]{:T(128)}, f32[2,8,128]{2,0,1:T(2,128)S(1)}, ...), condition=%wide.region_4.8_spmd, body=%wide.region_0.7_spmd.sunk | while | flops 567124544 | bytes 110340312 | solution.py:98
  130.4 11.6 %multiply_reduce_fusion.3 = (f32[32,8,128]{2,1,0:T(8,128)S(1)}, f32[32,8,128,128]{2,3,1,0:T(8,128)}) fusion(bf16[32,128,8,64]{1,3,2,0:T(8,128)(2,1)S(1)} %bitcast.185, bf16[32,128,8,64]{3,2,1,0:T(8,128)(2,1)} %broadcast_select_fusion.19), kind=kOutput, calls=%fused_computation.15.clone.1 | convolution fusion | flops 545226752 | bytes 25296896 | tf_op jit(solution)/shard_map/while/body/sihd,sjhd->shij/dot_general | solution.py:32
  142.8 10.7 %select_reduce_fusion.5 = f32[32,8,128]{2,1,0:T(8,128)S(1)} fusion(f32[32,8,128,128]{2,3,1,0:T(8,128)} %get-tuple-element.622, f32[32,8,128]{2,1,0:T(8,128)S(1)} %broadcast_select_fusion.20, pred[32]{0:T(512)(128)(4,1)S(1)} %get-tuple-element.621), kind=kLoop, calls=%fused_computation.14.clone.1 | loop fusion | flops 16744448 | bytes 17039392 | tf_op jit(solution)/shard_map/while/body/reduce_sum | solution.py:91
  153.9 91.2 %while.35 = (s32[]{:T(128)}, f32[2,128,8,64]{1,0,3,2:T(2,128)S(1)}, s32[]{:T(128)}, s32[32,2]{0,1:T(2,128)S(1)}, s32[]{:T(128)}, /*index=5*/bf16[16,128,1024]{2,...) while((s32[]{:T(128)}, f32[2,128,8,64]{1,0,3,2:T(2,128)S(1)}, ...), condition=%wide.region_6.10_spmd, body=%wide.region_5.9_spmd.sunk | while | flops 1151535744 | bytes 115615744 | solution.py:115
  201.8 14.4 %fusion.117 = f32[32,128,8,64]{1,3,2,0:T(8,128)} fusion(bf16[32,128,8,64]{1,3,2,0:T(8,128)(2,1)} %bitcast.190, bf16[32,128,8,64]{1,3,2,0:T(8,128)(2,1)} %bitcast.191, bf16[32,128,8,64]{3,2,1,0:T(8,128)(2,1)} %broadcast_select_fusion.22, f32[32,8,128]{2,1,0:T(8,128)S(1)} %get-tuple-element.638, f32[32,8,128]{2,1,0:T(8,128)S(1)} %get-tuple-element.639, ...), kind=kOutput, calls=%fused_computation.42.clone.2 | convolution fusion | flops 1094713344 | bytes 21233696 | tf_op jit(solution)/shard_map/while/body/shij,sjhd->sihd/dot_general | solution.py:108
  216.2 11.3 %fusion.118 = f32[2,128,8,64]{1,0,3,2:T(2,128)S(1)} fusion(f32[2,128,8,64]{1,0,3,2:T(2,128)S(1)} %get-tuple-element.709, f32[32,128,8,64]{1,3,2,0:T(8,128)} %fusion.117, pred[32]{0:T(512)(128)(4,1)S(1)} %get-tuple-element.640, s32[32]{0:T(128)S(1)} %slice_bitcast_fusion.8), kind=kOutput, calls=%fused_computation.43.clone.1 | convolution fusion | flops 50462848 | bytes 9437344 | tf_op jit(solution)/shard_map/while/body/sn,sihd->nihd/dot_general | solution.py:111
  250.7 199.1 %while.36 = (s32[]{:T(128)}, f32[2,128,8,64]{1,0,3,2:T(2,128)S(1)}, f32[16,128,1024]{2,1,0:T(8,128)}, s32[]{:T(128)}, s32[32,2]{0,1:T(2,128)S(1)}, /*index=5*/s3...) while((s32[]{:T(128)}, f32[2,128,8,64]{1,0,3,2:T(2,128)S(1)}, ...), condition=%wide.region_10.14_spmd, body=%wide.region_8.13_spmd.sunk | while | flops 2793639936 | bytes 384713920 | solution.py:168
  296.7 11.6 %broadcast_select_fusion.25 = (bf16[32,128,8,64]{3,2,1,0:T(8,128)(2,1)}, bf16[32,128,8,64]{3,2,1,0:T(8,128)(2,1)}) fusion(bf16[32,128,8,64]{3,2,1,0:T(8,128)(2,1)} %gather_fusion.8, pred[32]{0:T(512)(128)(4,1)S(1)} %get-tuple-element.657, bf16[32,128,8,64]{3,2,1,0:T(8,128)(2,1)} %gather_fusion.9), kind=kLoop, calls=%fused_computation.68.clone.1 | loop fusion | flops 4194304 | bytes 16777248 | tf_op jit(solution)/shard_map/while/body/jit(_take)/select_n | solution.py:133
  326.5 15.2 %select_convert_fusion.3 = bf16[32,8,128,128]{3,2,1,0:T(8,128)(2,1)S(1)} fusion(bf16[32,128,8,64]{1,3,2,0:T(8,128)(2,1)} %copy.232, bf16[32,128,8,64]{1,3,2,0:T(8,128)(2,1)} %bitcast.188, f32[32,8,128]{2,1,0:T(8,128)S(1)} %get-tuple-element.659, f32[32,8,128]{2,1,0:T(8,128)S(1)} %get-tuple-element.660, pred[32]{0:T(512)(128)(4,1)S(1)} %get-tuple-element.661), kind=kOutput, calls=%fused_computation.64.clone.1 | convolution fusion | flops 557842432 | bytes 17039392 | tf_op jit(solution)/shard_map/while/body/sihd,sjhd->shij/dot_general | solution.py:32
  364.0 10.2 %broadcast_multiply_fusion.2 = f32[32,8,64,128]{3,2,1,0:T(8,128)} fusion(bf16[32,128,8,64]{1,3,2,0:T(8,128)(2,1)} %copy.232, bf16[32,8,128,128]{3,2,1,0:T(8,128)(2,1)} %multiply_convert_fusion.2), kind=kOutput, calls=%fused_computation.71.clone.1 | convolution fusion | flops 538968064 | bytes 20971520 | tf_op jit(solution)/shard_map/while/body/shij,sihd->sjhd/dot_general | solution.py:149
  374.2 10.5 %multiply_bitcast_fusion.2 = f32[32,128,8,64]{1,3,2,0:T(8,128)S(1)} fusion(bf16[32,128,8,64]{1,3,2,0:T(8,128)(2,1)} %bitcast.189, bf16[32,8,128,128]{3,2,1,0:T(8,128)(2,1)} %multiply_convert_fusion.2), kind=kOutput, calls=%fused_computation.67.clone.1 | convolution fusion | flops 538968064 | bytes 20971520 | tf_op jit(solution)/shard_map/while/body/shij,sjhd->sihd/dot_general | solution.py:145
  402.2 11.7 %pad_maximum_fusion.3 = f32[32,128,1024]{2,1,0:T(8,128)} fusion(f32[32,128,512]{2,1,0:T(8,128)} %copy.235, f32[32,128,512]{2,1,0:T(8,128)} %copy.236), kind=kLoop, calls=%fused_computation.62.clone.1 | loop fusion | flops 4194304 | bytes 33554432 | tf_op jit(solution)/shard_map/while/body/concatenate | solution.py:157
  413.9 35.7 %scatter_fusion = f32[16,128,1024]{2,1,0:T(8,128)} fusion(f32[16,128,1024]{2,1,0:T(8,128)} %get-tuple-element.746, s32[32]{0:T(128)S(1)} %get-tuple-element.666, f32[32,128,1024]{2,1,0:T(8,128)} %pad_maximum_fusion.3), kind=kCustom, calls=%fused_computation.13.clone.1 | custom fusion | flops 4194304 | bytes 50331776 | tf_op jit(solution)/shard_map/while/body/scatter-add | solution.py:161
  458.5 46.2 %reduce-scatter.12.cloned.1.call-done = bf16[256,1024]{1,0:T(8,128)(2,1)} async-done(((bf16[2048,1024]{1,0:T(8,128)(2,1)}), bf16[256,1024]{1,0:T(8,128)(2,1)}) %reduce-scatter.12.cloned.1.call-update) | async-done | bytes 524304 | tf_op jit(solution)/shard_map/reduce_scatter | solution.py:170
  514.8 22.9 %reduce-scatter.16.cloned.1.call-done = bf16[128,512]{1,0:T(8,128)(2,1)} async-done(((bf16[1024,512]{1,0:T(8,128)(2,1)}), bf16[128,512]{1,0:T(8,128)(2,1)}) %reduce-scatter.16.cloned.1.call-update) | async-done | bytes 131088
  539.5 13.7 %reduce-scatter.14.cloned.1.call-done = bf16[256,512]{1,0:T(8,128)(2,1)} async-done(((bf16[256,1024]{1,0:T(8,128)(2,1)}), bf16[256,512]{1,0:T(8,128)(2,1)}) %reduce-scatter.14.cloned.1.call-update) | async-done | bytes 262160 | tf_op jit(solution)/shard_map/reduce_scatter | solution.py:186
  555.0 32.9 %reduce-scatter.18.cloned.1.call-done = bf16[128,512]{1,0:T(8,128)(2,1)} async-done(((bf16[1024,512]{1,0:T(8,128)(2,1)}), bf16[128,512]{1,0:T(8,128)(2,1)}) %reduce-scatter.18.cloned.1.call-update) | async-done | bytes 131088
  589.7 31.0 %reduce-scatter.20.cloned.1.call-done = bf16[128,512]{1,0:T(8,128)(2,1)} async-done(((bf16[1024,512]{1,0:T(8,128)(2,1)}), bf16[128,512]{1,0:T(8,128)(2,1)}) %reduce-scatter.20.cloned.1.call-update) | async-done | bytes 131088
  (172 shorter events, 243.3 us)
Async XLA Ops:
  7.2 71.7 %copy-start = (bf16[1024,512]{1,0:T(8,128)(2,1)S(1)}, bf16[1024,512]{1,0:T(8,128)(2,1)}, u32[]{:S(2)}) copy-start(bf16[1024,512]{1,0:T(8,128)(2,1)} %param.20) | copy-start | bytes 3145732
  7.2 239.1 %all-gather.2.cloned.1.call-start = ((), (), s32[]{:S(2)}) async-start(), calls=%async_computation.5 | async-start | bytes 4718592 | tf_op jit(solution)/shard_map/all_gather | solution.py:121
  11.0 65.9 %copy-start.8 = (bf16[256,1024]{1,0:T(8,128)(2,1)}, bf16[256,1024]{1,0:T(8,128)(2,1)S(1)}, u32[]{:S(2)}) copy-start(bf16[256,1024]{1,0:T(8,128)(2,1)S(1)} %pad_maximum_fusion.1) | copy-start | bytes 1572868
  11.0 11.4 %collective-permute-start = (bf16[256,1024]{1,0:T(8,128)(2,1)S(1)}, bf16[256,1024]{1,0:T(8,128)(2,1)S(1)}, u32[]{:S(2)}, u32[]{:S(2)}) collective-permute-start(bf16[256,1024]{1,0:T(8,128)(2,1)S(1)} %pad_maximum_fusion.1), channel_id=1, source_target_pairs={{0,1},{1,2},{2,3},{3,4},{4,5},{5,6},{6,7},{7,0},{8,9},{9,10},{10,1... | collective-permute-start | bytes 1572872 | tf_op jit(solution)/shard_map/ppermute | solution.py:69
  22.4 10.4 %collective-permute-start.1 = (bf16[256,1024]{1,0:T(8,128)(2,1)S(1)}, bf16[256,1024]{1,0:T(8,128)(2,1)S(1)}, u32[]{:S(2)}, u32[]{:S(2)}) collective-permute-start(bf16[256,1024]{1,0:T(8,128)(2,1)S(1)} %collective-permute-done), channel_id=1, source_target_pairs={{0,1},{1,2},{2,3},{3,4},{4,5},{5,6},{6,7},{7,0},{8,9},{9,10},{10,1... | collective-permute-start | bytes 1572872 | tf_op jit(solution)/shard_map/ppermute | solution.py:69
  32.8 10.4 %collective-permute-start.2 = (bf16[256,1024]{1,0:T(8,128)(2,1)S(1)}, bf16[256,1024]{1,0:T(8,128)(2,1)S(1)}, u32[]{:S(2)}, u32[]{:S(2)}) collective-permute-start(bf16[256,1024]{1,0:T(8,128)(2,1)S(1)} %collective-permute-done.1), channel_id=1, source_target_pairs={{0,1},{1,2},{2,3},{3,4},{4,5},{5,6},{6,7},{7,0},{8,9},{9,10},{10,1... | collective-permute-start | bytes 1572872 | tf_op jit(solution)/shard_map/ppermute | solution.py:69
  44.0 10.4 %collective-permute-start.3 = (bf16[256,1024]{1,0:T(8,128)(2,1)S(1)}, bf16[256,1024]{1,0:T(8,128)(2,1)S(1)}, u32[]{:S(2)}, u32[]{:S(2)}) collective-permute-start(bf16[256,1024]{1,0:T(8,128)(2,1)S(1)} %collective-permute-done.2), channel_id=1, source_target_pairs={{0,1},{1,2},{2,3},{3,4},{4,5},{5,6},{6,7},{7,0},{8,9},{9,10},{10,1... | collective-permute-start | bytes 1572872 | tf_op jit(solution)/shard_map/ppermute | solution.py:69
  55.2 10.4 %collective-permute-start.4 = (bf16[256,1024]{1,0:T(8,128)(2,1)S(1)}, bf16[256,1024]{1,0:T(8,128)(2,1)S(1)}, u32[]{:S(2)}, u32[]{:S(2)}) collective-permute-start(bf16[256,1024]{1,0:T(8,128)(2,1)S(1)} %collective-permute-done.3), channel_id=1, source_target_pairs={{0,1},{1,2},{2,3},{3,4},{4,5},{5,6},{6,7},{7,0},{8,9},{9,10},{10,1... | collective-permute-start | bytes 1572872 | tf_op jit(solution)/shard_map/ppermute | solution.py:69
  66.4 10.5 %collective-permute-start.5 = (bf16[256,1024]{1,0:T(8,128)(2,1)S(1)}, bf16[256,1024]{1,0:T(8,128)(2,1)}, u32[]{:S(2)}, u32[]{:S(2)}) collective-permute-start(bf16[256,1024]{1,0:T(8,128)(2,1)S(1)} %collective-permute-done.4), channel_id=1, source_target_pairs={{0,1},{1,2},{2,3},{3,4},{4,5},{5,6},{6,7},{7,0},{8,9},{9,10},{10,1... | collective-permute-start | bytes 1572872 | tf_op jit(solution)/shard_map/ppermute | solution.py:69
  76.9 10.7 %collective-permute-start.6 = (bf16[256,1024]{1,0:T(8,128)(2,1)}, bf16[256,1024]{1,0:T(8,128)(2,1)}, u32[]{:S(2)}, u32[]{:S(2)}) collective-permute-start(bf16[256,1024]{1,0:T(8,128)(2,1)} %collective-permute-done.5), channel_id=1, source_target_pairs={{0,1},{1,2},{2,3},{3,4},{4,5},{5,6},{6,7},{7,0},{8,9},{9,10},{10,1... | collective-permute-start | bytes 1572872 | tf_op jit(solution)/shard_map/ppermute | solution.py:69
  77.0 427.7 %reduce-scatter.12.cloned.1.call-start = ((), (), s32[]{:S(2)}) async-start(), calls=%async_computation.6 | async-start | bytes 4718592 | tf_op jit(solution)/shard_map/reduce_scatter | solution.py:170
  78.9 16.7 %copy-start.6 = (bf16[2,128,8,64]{1,0,3,2:T(2,128)(2,1)}, bf16[2,128,8,64]{1,0,3,2:T(2,128)(2,1)S(1)}, u32[]{:S(2)}) copy-start(bf16[2,128,8,64]{1,0,3,2:T(2,128)(2,1)S(1)} %reshape.145) | copy-start | bytes 786436
  83.5 11.9 %copy-start.14 = (bf16[256,1024]{1,0:T(8,128)(2,1)S(1)}, bf16[256,1024]{1,0:T(8,128)(2,1)}, u32[]{:S(2)}) copy-start(bf16[256,1024]{1,0:T(8,128)(2,1)} %copy-done.13) | copy-start | bytes 1572868
  83.5 12.0 %copy-start.12 = (bf16[256,1024]{1,0:T(8,128)(2,1)S(1)}, bf16[256,1024]{1,0:T(8,128)(2,1)}, u32[]{:S(2)}) copy-start(bf16[256,1024]{1,0:T(8,128)(2,1)} %copy-done.11) | copy-start | bytes 1572868
  83.5 12.0 %copy-start.10 = (bf16[256,1024]{1,0:T(8,128)(2,1)S(1)}, bf16[256,1024]{1,0:T(8,128)(2,1)}, u32[]{:S(2)}) copy-start(bf16[256,1024]{1,0:T(8,128)(2,1)} %copy-done.9) | copy-start | bytes 1572868
  153.9 91.3 %copy-start.7 = (bf16[2,128,8,64]{1,0,3,2:T(2,128)(2,1)S(1)}, bf16[2,128,8,64]{1,0,3,2:T(2,128)(2,1)}, u32[]{:S(2)}) copy-start(bf16[2,128,8,64]{1,0,3,2:T(2,128)(2,1)} %copy-done.6) | copy-start | bytes 786436
  326.5 15.2 %copy-start.2 = (bf16[32,128,8,64]{1,3,2,0:T(8,128)(2,1)S(1)}, bf16[32,128,8,64]{1,3,2,0:T(8,128)(2,1)}, u32[]{:S(2)}) copy-start(bf16[32,128,8,64]{1,3,2,0:T(8,128)(2,1)} %copy.233) | copy-start | bytes 12582916 | tf_op jit(solution)/shard_map/while
  326.5 15.2 %copy-start.4 = (bf16[32,128,512]{1,2,0:T(8,128)(2,1)S(1)}, bf16[32,128,512]{1,2,0:T(8,128)(2,1)}, u32[]{:S(2)}) copy-start(bf16[32,128,512]{1,2,0:T(8,128)(2,1)} %copy.234) | copy-start | bytes 12582916 | tf_op jit(solution)/shard_map/while
  413.9 35.7 %copy-start.19 = (s32[32,2]{0,1:T(2,128)S(1)}, s32[32,2]{0,1:T(2,128)}, u32[]{:S(2)}) copy-start(s32[32,2]{0,1:T(2,128)} %copy-done.18) | copy-start | bytes 772 | tf_op jit(solution)/shard_map/while
  455.9 81.7 %reduce-scatter.16.cloned.1.call-start = ((), (), s32[]{:S(2)}) async-start(), calls=%async_computation.8 | async-start | bytes 1179648
  457.9 95.2 %reduce-scatter.14.cloned.1.call-start = ((), (), s32[]{:S(2)}) async-start(), calls=%async_computation.7 | async-start | bytes 786432 | tf_op jit(solution)/shard_map/reduce_scatter | solution.py:186
  458.5 55.4 %copy-start.16 = (bf16[2,128,8,64]{1,0,3,2:T(2,128)(2,1)S(1)}, bf16[2,128,8,64]{1,0,3,2:T(2,128)(2,1)}, u32[]{:S(2)}) copy-start(bf16[2,128,8,64]{1,0,3,2:T(2,128)(2,1)} %get-tuple-element.426) | copy-start | bytes 786436
  509.1 78.7 %reduce-scatter.18.cloned.1.call-start = ((), (), s32[]{:S(2)}) async-start(), calls=%async_computation.9 | async-start | bytes 1179648
  512.0 108.7 %reduce-scatter.20.cloned.1.call-start = ((), (), s32[]{:S(2)}) async-start(), calls=%async_computation.10 | async-start | bytes 1179648
  (9 other events, 44.2 us)
Sparse Core Ops, SparseCore 0:
  77.1 48.8 all-gather.1
  456.0 48.6 reduce-scatter.11
  507.0 30.5 reduce-scatter.15
  540.3 12.8 reduce-scatter.13
  555.4 32.4 reduce-scatter.17
  590.1 30.5 reduce-scatter.19
